TPU v7x, 32 devices: a whole 2x2x4 slice. The times are simulated.
32 devices in a mesh: gx: 8 (over z, core), gy: 4 (over y, x).
Axes of the slice: x: 2, y: 2, z: 4, core: 2. Of those that a mesh axis runs over, the one named last changes fastest.
Arguments:
- adj_voltage: float32 [8, 256, 128], P('gx', 'gy'), may hold values from -6 to 6
- adj_gating: float32 [8, 256, 128], P('gx', 'gy'), may hold values from -1.2 to 1.2
- fwd_voltage: bfloat16 [2, 8, 256, 128], P(None, 'gx', 'gy'), may hold values from -0.099609375 to 1.09375
- fwd_gating: bfloat16 [2, 8, 256, 128], P(None, 'gx', 'gy'), may hold values from 0 to 2
- region_labels: int32 [8, 256, 1], P('gx', 'gy'), may hold values from 0 to 7
- region_axial: float32 [2, 8], replicated, may hold values from 0.6 to 3
- region_shear: float32 [8], replicated, may hold values from -0.5 to 0.5
- block_rate: float32 [2], replicated, may hold values from 8 to 32
- block_inverse: float32 [2, 128, 128], replicated, as said below
Outputs:
- voltage_adjoint: float32 [8, 256, 128], P('gx', 'gy')
- gating_adjoint: float32 [8, 256, 128], P('gx', 'gy')
Inputs may be any that keep to these rules, and one draw needn't show every extreme that they name: block_inverse[b] is the inverse of the 128 x 128 tridiagonal matrix with diagonal 1 + 2 block_rate[b] and off-diagonals -block_rate[b].
All inputs are finite; a program needn't handle non-finite values.
Results may differ from a plain program's by a relative error of at most 0.00065.
Values sent between devices are 32-bit elements; how exact they have to be, the bound alone decides.
No kernel may reach another device: no remote copies, remote signals or barrier semaphores. Data moves between devices by JAX's collectives and lax.ppermute only.
A program may use at most 64 MiB of HBM per device.

v0:
```python
import jax
import jax.numpy as jnp
from jax import lax
from jax.sharding import PartitionSpec as P

STEPS = 2
SWEEPS = 11
ZB = 128
LB = 128
FULL_PRECISION = lax.Precision.HIGHEST
TIME_STEP = 0.2
RECOVERY_RATE = 0.25
EXCITATION = 8.0
THRESHOLD = 0.15


def with_halo(x, sides, width):
    for axis, dim in sides:
        size, length = (lax.axis_size(axis), x.shape[dim])
        up = [(i, (i + 1) % size) for i in range(size - 1)]
        down = [(j, i) for i, j in up]
        last = lax.slice_in_dim(x, length - width, length, axis=dim)
        leading = lax.slice_in_dim(x, 0, width, axis=dim)
        before = lax.ppermute(last, axis, up)
        after = lax.ppermute(leading, axis, down)
        x = jnp.concatenate([before, x, after], axis=dim)
    return x


def lookup(labels, lookup_table):
    levels = jnp.arange(lookup_table.shape[0], dtype=jnp.int32)
    return jnp.sum(jnp.where(labels[..., None] == levels, lookup_table, 0.0), axis=-1)


def expand_blocks(block_values):
    block_shape = block_values.shape
    wide_form = jnp.broadcast_to(block_values[..., None], block_shape + (LB,))
    return wide_form.reshape(block_shape[0], block_shape[1], block_shape[2] * LB)


def coefficients(labels, region_axial, region_shear):
    tissue_block = (labels > 0).astype(jnp.float32)
    return (
        expand_blocks(tissue_block),
        expand_blocks(lookup(labels, region_axial[0]) * tissue_block),
        expand_blocks(lookup(labels, region_axial[1]) * tissue_block),
        expand_blocks(lookup(labels, region_shear) * tissue_block),
    )


def couplings(block_rate):
    zero_rate = jnp.zeros((1,), jnp.float32)
    inner_rate = jnp.minimum(block_rate[:-1], block_rate[1:])
    return (jnp.concatenate([zero_rate, inner_rate]), jnp.concatenate([inner_rate, zero_rate]))


def line_solve(line_cells, block_rate, block_inverse):
    item_count, length_cells, across = line_cells.shape
    blocks_count = length_cells // ZB
    shaped = line_cells.reshape(item_count, blocks_count, ZB, across)
    below_rate, after_rate = couplings(block_rate)
    base_blocks = jnp.einsum("bij,xbjy->xbiy", block_inverse, shaped, precision=FULL_PRECISION)
    zero_row = jnp.zeros((item_count, 1, across), jnp.float32)
    middle = jnp.zeros((item_count, blocks_count, ZB - 2, across), jnp.float32)

    def sweep_once(sweep_index, current):
        first_cells = current[:, :, 0, :]
        last_cells = current[:, :, ZB - 1, :]
        from_below = (
            jnp.concatenate([zero_row, last_cells[:, :-1, :]], axis=1) * below_rate[None, :, None]
        )
        from_above = (
            jnp.concatenate([first_cells[:, 1:, :], zero_row], axis=1) * after_rate[None, :, None]
        )
        coupling = jnp.concatenate(
            [from_below[:, :, None, :], middle, from_above[:, :, None, :]], axis=2
        )
        updated = jnp.einsum(
            "bij,xbjy->xbiy", block_inverse, shaped + coupling, precision=FULL_PRECISION
        )
        return updated

    current = lax.fori_loop(0, SWEEPS, sweep_once, base_blocks)
    return current.reshape(item_count, length_cells, across)


def cross_terms(ext_xx, ext_yy, ext_xy):
    pad_y = ((0, 0), (0, 0), (1, 1))
    ext_yy = jnp.pad(ext_yy, pad_y)
    ext_xy = jnp.pad(ext_xy, pad_y)
    term_xx = ext_xx[2:] - 2.0 * ext_xx[1:-1] + ext_xx[:-2]
    term_yy = ext_yy[1:-1, :, 2:] - 2.0 * ext_yy[1:-1, :, 1:-1] + ext_yy[1:-1, :, :-2]
    term_xy = (
        ext_xy[2:, :, 2:] - ext_xy[2:, :, :-2] - ext_xy[:-2, :, 2:] + ext_xy[:-2, :, :-2]
    ) * 0.25
    return term_xx + term_yy + 2.0 * term_xy


def per_device(
    adj_voltage,
    adj_gating,
    fwd_voltage,
    fwd_gating,
    region_labels,
    region_axial,
    region_shear,
    block_rate,
    block_inverse,
):
    groups = lax.axis_size("gy")
    row_count, depth_cells, width_cells = adj_voltage.shape
    narrow = width_cells // groups
    tissue, coef_xx, coef_yy, coef_xy = coefficients(region_labels, region_axial, region_shear)
    adjoint_v = adj_voltage
    adjoint_w = adj_gating
    for step_index in range(STEPS):
        later_index = STEPS - 1 - step_index
        outgoing = adjoint_v.reshape(row_count, 1, depth_cells, groups, narrow)
        pieces = lax.all_to_all(outgoing, "gy", split_axis=3, concat_axis=1, tiled=True)
        item_count = pieces.shape[0]
        line_cells = pieces.reshape(item_count, groups * depth_cells, narrow)
        solved_lines = line_solve(line_cells, block_rate, block_inverse)
        returned_form = solved_lines.reshape(item_count, groups, depth_cells, 1, narrow)
        returned = lax.all_to_all(returned_form, "gy", split_axis=1, concat_axis=3, tiled=True)
        solved = returned.reshape(item_count, depth_cells, width_cells)
        stacked = jnp.stack([coef_xx * solved, coef_yy * solved, coef_xy * solved])
        extended = with_halo(stacked, (("gx", 1),), 1)
        spread_term = cross_terms(extended[0], extended[1], extended[2])
        voltage_now = fwd_voltage[later_index].astype(jnp.float32)
        gating_now = fwd_gating[later_index].astype(jnp.float32)
        ionic_slope = (
            EXCITATION
            * (-3.0 * voltage_now * voltage_now + 2.0 * (1.0 + THRESHOLD) * voltage_now - THRESHOLD)
            - gating_now
        )
        next_v = tissue * (
            solved
            + TIME_STEP * spread_term
            + TIME_STEP * ionic_slope * solved
            + TIME_STEP * RECOVERY_RATE * EXCITATION * adjoint_w
        )
        adjoint_w = tissue * (
            (1.0 - TIME_STEP * RECOVERY_RATE) * adjoint_w - TIME_STEP * voltage_now * solved
        )
        adjoint_v = next_v
    return (adjoint_v, adjoint_w)


def solution(mesh):
    return jax.shard_map(
        per_device,
        mesh=mesh,
        in_specs=(
            P("gx", "gy", None),
            P("gx", "gy", None),
            P(None, "gx", "gy", None),
            P(None, "gx", "gy", None),
            P("gx", "gy", None),
            P(),
            P(),
            P(),
            P(),
        ),
        out_specs=(P("gx", "gy", None), P("gx", "gy", None)),
        check_vma=False,
    )
```

profile of v0, /device:TPU:1, one launch (start us, length us, event | category | flops | bytes accessed | tf_op | source)
XLA Modules:
  0.0 79.6 jit_solution(2943020983780482412)
XLA Ops:
  0.6 0.8 %copy.73 = f32[1,64,128]{1,2,0:T(8,128)S(1)} copy(f32[1,64,128]{2,1,0:T(8,128)} %param.13) | data formatting | bytes 65536 | tf_op args[0]
  1.5 0.7 reshape.981
  2.2 4.4 %all-to-all-start = ((f32[4,1,2048]{2,1,0:T(1,128)}), f32[4,1,2048]{2,1,0:T(1,128)S(1)}, u32[]{:S(2)}, u32[]{:S(2)}) async-start(f32[4,1,2048]{2,1,0:T(1,128)} %reshape.981), calls=%async_computation | async-start | bytes 65536 | tf_op jit(solution)/shard_map/all_to_all | solution.py:119
  6.6 0.6 fusion.69
  7.3 0.7 copy-done.3
  9.4 0.6 copy-done.4
  10.2 0.5 broadcast.556
  10.7 0.7 reduce.11
  11.9 0.7 copy-done
  12.5 0.3 convolution_bitcast_fusion.3
  12.8 9.9 %while.20 = (s32[]{:T(128)}, f32[1,2,128,32]{2,3,1,0:T(8,128)S(1)}, f32[1,2,128,32]{2,3,1,0:T(8,128)S(1)}, f32[2]{0:T(128)S(1)}, f32[2]{0:T(128)S(1)}, /*index=5...) while((s32[]{:T(128)}, f32[1,2,128,32]{2,3,1,0:T(8,128)S(1)}, f32[1,2,128,32]{2,3,1,0:T(8,128)S(1)}, ...), condition=%wide.region_1.2_spmd, body=%wide.region_0.1_spmd.sunk | while | flops 12607618 | bytes 202597 | solution.py:83
  12.8 0.2 slice_reduce_fusion.6
  13.4 0.4 convolution_bitcast_fusion.6
  14.3 0.4 convolution_bitcast_fusion.6
  14.6 0.2 slice_reduce_fusion.6
  15.2 0.4 convolution_bitcast_fusion.6
  15.5 0.2 slice_reduce_fusion.6
  16.1 0.4 convolution_bitcast_fusion.6
  17.0 0.4 convolution_bitcast_fusion.6
  17.4 0.2 slice_reduce_fusion.6
  17.9 0.4 convolution_bitcast_fusion.6
  18.3 0.2 slice_reduce_fusion.6
  18.8 0.4 convolution_bitcast_fusion.6
  19.2 0.2 slice_reduce_fusion.6
  19.7 0.4 convolution_bitcast_fusion.6
  20.1 0.2 slice_reduce_fusion.6
  20.6 0.4 convolution_bitcast_fusion.6
  21.0 0.2 slice_reduce_fusion.6
  21.5 0.4 convolution_bitcast_fusion.6
  21.9 0.2 slice_reduce_fusion.6
  22.4 0.4 convolution_bitcast_fusion.6
  22.9 0.7 reshape.983
  23.6 3.6 %all-to-all-start.1 = ((f32[4,1,2048]{2,1,0:T(1,128)}), f32[4,1,2048]{2,1,0:T(1,128)S(1)}, u32[]{:S(2)}, u32[]{:S(2)}) async-start(f32[4,1,2048]{2,1,0:T(1,128)} %reshape.983), calls=%async_computation.1 | async-start | bytes 65536 | tf_op jit(solution)/shard_map/all_to_all | solution.py:124
  27.3 3.6 %all-to-all-done.1 = f32[4,1,2048]{2,1,0:T(1,128)S(1)} async-done(((f32[4,1,2048]{2,1,0:T(1,128)}), f32[4,1,2048]{2,1,0:T(1,128)S(1)}, u32[]{:S(2)}, u32[]{:S(2)}) %all-to-all-start.1) | async-done | bytes 32800 | tf_op jit(solution)/shard_map/all_to_all | solution.py:124
  30.9 0.7 reduce.12
  31.7 4.8 %collective-permute-start = (f32[3,1,64,128]{2,3,1,0:T(8,128)S(1)}, f32[3,1,64,128]{2,3,1,0:T(8,128)S(1)}, u32[]{:S(2)}, u32[]{:S(2)}) collective-permute-start(f32[3,1,64,128]{2,3,1,0:T(8,128)S(1)} %pad_maximum_fusion.8), channel_id=1, source_target_pairs={{4,0},{8,4},{12,8},{16,12},{20,16},{24,20},{28,24},{5,1},{9,5},{13... | collective-permute-start | bytes 294920 | tf_op jit(solution)/shard_map/ppermute | solution.py:25
  36.5 3.1 %collective-permute-start.1 = (f32[3,1,64,128]{2,3,1,0:T(8,128)S(1)}, f32[3,1,64,128]{2,3,1,0:T(8,128)S(1)}, u32[]{:S(2)}, u32[]{:S(2)}) collective-permute-start(f32[3,1,64,128]{2,3,1,0:T(8,128)S(1)} %pad_maximum_fusion.8), channel_id=1, source_target_pairs={{0,4},{4,8},{8,12},{12,16},{16,20},{20,24},{24,28},{1,5},{5,9},{9,... | collective-permute-start | bytes 294920 | tf_op jit(solution)/shard_map/ppermute | solution.py:24
  39.9 0.6 copy-done.1
  40.6 0.4 collective-permute-done
  41.0 1.2 %collective-permute-done.1 = f32[3,1,64,128]{2,3,1,0:T(8,128)S(1)} collective-permute-done((f32[3,1,64,128]{2,3,1,0:T(8,128)S(1)}, f32[3,1,64,128]{2,3,1,0:T(8,128)S(1)}, u32[]{:S(2)}, u32[]{:S(2)}) %collective-permute-start.1) | collective-permute-done | bytes 98336 | tf_op jit(solution)/shard_map/ppermute | solution.py:24
  42.5 6.0 %all_to_all.60 = f32[4,1,2048]{2,1,0:T(1,128)S(1)} all-to-all(f32[4,1,2048]{2,1,0:T(1,128)S(1)} %reshape.985), channel_id=1, replica_groups=mesh['gx'=8,'gy'=4] {'gy'}, dimensions={0} | all-to-all | bytes 65536 | tf_op jit(solution)/shard_map/all_to_all | solution.py:119
  48.4 0.7 reduce.13
  49.5 0.3 convolution_bitcast_fusion.2
  49.8 9.9 %while.21 = (s32[]{:T(128)}, f32[1,2,128,32]{2,3,1,0:T(8,128)S(1)}, f32[1,2,128,32]{2,3,1,0:T(8,128)S(1)}, f32[2]{0:T(128)S(1)}, f32[2]{0:T(128)S(1)}, /*index=5...) while((s32[]{:T(128)}, f32[1,2,128,32]{2,3,1,0:T(8,128)S(1)}, f32[1,2,128,32]{2,3,1,0:T(8,128)S(1)}, ...), condition=%wide.region_6.7_spmd, body=%wide.region_5.6_spmd.sunk | while | flops 12607618 | bytes 202597 | solution.py:83
  50.4 0.4 convolution_bitcast_fusion.7
  51.3 0.4 convolution_bitcast_fusion.7
  51.6 0.2 slice_reduce_fusion.7
  52.2 0.4 convolution_bitcast_fusion.7
  53.1 0.4 convolution_bitcast_fusion.7
  54.0 0.4 convolution_bitcast_fusion.7
  54.9 0.4 convolution_bitcast_fusion.7
  55.8 0.4 convolution_bitcast_fusion.7
  56.7 0.4 convolution_bitcast_fusion.7
  57.6 0.4 convolution_bitcast_fusion.7
  58.5 0.4 convolution_bitcast_fusion.7
  59.4 0.4 convolution_bitcast_fusion.7
  60.0 6.0 %all_to_all.61 = f32[4,1,2048]{2,1,0:T(1,128)S(1)} all-to-all(f32[4,1,2048]{2,1,0:T(1,128)S(1)} %reshape.987), channel_id=1, replica_groups=mesh['gx'=8,'gy'=4] {'gy'}, dimensions={0} | all-to-all | bytes 65536 | tf_op jit(solution)/shard_map/all_to_all | solution.py:124
  66.0 0.7 reduce.14
  66.8 2.0 %collective-permute-start.2 = (f32[3,1,64,128]{2,3,1,0:T(8,128)S(1)}, f32[3,1,64,128]{2,3,1,0:T(8,128)S(1)}, u32[]{:S(2)}, u32[]{:S(2)}) collective-permute-start(f32[3,1,64,128]{2,3,1,0:T(8,128)S(1)} %pad_maximum_fusion.9), channel_id=1, source_target_pairs={{4,0},{8,4},{12,8},{16,12},{20,16},{24,20},{28,24},{5,1},{9,5},{13... | collective-permute-start | bytes 294920 | tf_op jit(solution)/shard_map/ppermute | solution.py:25
  68.8 6.6 %collective-permute-start.3 = (f32[3,1,64,128]{2,3,1,0:T(8,128)S(1)}, f32[3,1,64,128]{2,3,1,0:T(8,128)S(1)}, u32[]{:S(2)}, u32[]{:S(2)}) collective-permute-start(f32[3,1,64,128]{2,3,1,0:T(8,128)S(1)} %pad_maximum_fusion.9), channel_id=1, source_target_pairs={{0,4},{4,8},{8,12},{12,16},{16,20},{20,24},{24,28},{1,5},{5,9},{9,... | collective-permute-start | bytes 294920 | tf_op jit(solution)/shard_map/ppermute | solution.py:24
  75.7 1.2 %collective-permute-done.2 = f32[3,1,64,128]{2,3,1,0:T(8,128)S(1)} collective-permute-done((f32[3,1,64,128]{2,3,1,0:T(8,128)S(1)}, f32[3,1,64,128]{2,3,1,0:T(8,128)S(1)}, u32[]{:S(2)}, u32[]{:S(2)}) %collective-permute-start.2) | collective-permute-done | bytes 98336 | tf_op jit(solution)/shard_map/ppermute | solution.py:25
  76.9 1.2 %collective-permute-done.3 = f32[3,1,64,128]{2,3,1,0:T(8,128)S(1)} collective-permute-done((f32[3,1,64,128]{2,3,1,0:T(8,128)S(1)}, f32[3,1,64,128]{2,3,1,0:T(8,128)S(1)}, u32[]{:S(2)}, u32[]{:S(2)}) %collective-permute-start.3) | collective-permute-done | bytes 98336 | tf_op jit(solution)/shard_map/ppermute | solution.py:24
  78.2 0.7 copy.94
  78.9 0.7 copy.95
  (221 shorter events, 12.2 us)
Async XLA Ops:
  2.2 4.4 %copy-start.5 = (f32[2]{0:T(128)S(1)}, f32[2]{0:T(128)}, u32[]{:S(2)}) copy-start(f32[2]{0:T(128)} %param.20) | copy-start | bytes 28
  2.2 5.1 %copy-start.2 = (bf16[2,1,64,128]{3,2,1,0:T(8,128)(2,1)S(1)}, bf16[2,1,64,128]{3,2,1,0:T(8,128)(2,1)}, u32[]{:S(2)}) copy-start(bf16[2,1,64,128]{3,2,1,0:T(8,128)(2,1)} %param.15) | copy-start | bytes 98308
  2.2 8.0 %all-to-all-start = ((f32[4,1,2048]{2,1,0:T(1,128)}), f32[4,1,2048]{2,1,0:T(1,128)S(1)}, u32[]{:S(2)}, u32[]{:S(2)}) async-start(f32[4,1,2048]{2,1,0:T(1,128)} %reshape.981), calls=%async_computation | async-start | bytes 65536 | tf_op jit(solution)/shard_map/all_to_all | solution.py:119
  6.6 0.7 copy-start.6
  7.3 0.8 copy-start.3
  9.3 0.7 copy-start.4
  9.4 0.7 copy-start.7
  11.6 0.9 %copy-start = (f32[2,128,128]{2,1,0:T(8,128)S(1)}, f32[2,128,128]{2,1,0:T(8,128)}, u32[]{:S(2)}) copy-start(f32[2,128,128]{2,1,0:T(8,128)} %param.21) | copy-start | bytes 393220
  23.6 7.2 %all-to-all-start.1 = ((f32[4,1,2048]{2,1,0:T(1,128)}), f32[4,1,2048]{2,1,0:T(1,128)S(1)}, u32[]{:S(2)}, u32[]{:S(2)}) async-start(f32[4,1,2048]{2,1,0:T(1,128)} %reshape.983), calls=%async_computation.1 | async-start | bytes 65536 | tf_op jit(solution)/shard_map/all_to_all | solution.py:124
  31.7 9.3 %collective-permute-start = (f32[3,1,64,128]{2,3,1,0:T(8,128)S(1)}, f32[3,1,64,128]{2,3,1,0:T(8,128)S(1)}, u32[]{:S(2)}, u32[]{:S(2)}) collective-permute-start(f32[3,1,64,128]{2,3,1,0:T(8,128)S(1)} %pad_maximum_fusion.8), channel_id=1, source_target_pairs={{4,0},{8,4},{12,8},{16,12},{20,16},{24,20},{28,24},{5,1},{9,5},{13... | collective-permute-start | bytes 294920 | tf_op jit(solution)/shard_map/ppermute | solution.py:25
  36.5 5.7 %collective-permute-start.1 = (f32[3,1,64,128]{2,3,1,0:T(8,128)S(1)}, f32[3,1,64,128]{2,3,1,0:T(8,128)S(1)}, u32[]{:S(2)}, u32[]{:S(2)}) collective-permute-start(f32[3,1,64,128]{2,3,1,0:T(8,128)S(1)} %pad_maximum_fusion.8), channel_id=1, source_target_pairs={{0,4},{4,8},{8,12},{12,16},{16,20},{20,24},{24,28},{1,5},{5,9},{9,... | collective-permute-start | bytes 294920 | tf_op jit(solution)/shard_map/ppermute | solution.py:24
  39.8 0.8 copy-start.1
  66.8 10.0 %collective-permute-start.2 = (f32[3,1,64,128]{2,3,1,0:T(8,128)S(1)}, f32[3,1,64,128]{2,3,1,0:T(8,128)S(1)}, u32[]{:S(2)}, u32[]{:S(2)}) collective-permute-start(f32[3,1,64,128]{2,3,1,0:T(8,128)S(1)} %pad_maximum_fusion.9), channel_id=1, source_target_pairs={{4,0},{8,4},{12,8},{16,12},{20,16},{24,20},{28,24},{5,1},{9,5},{13... | collective-permute-start | bytes 294920 | tf_op jit(solution)/shard_map/ppermute | solution.py:25
  68.8 9.2 %collective-permute-start.3 = (f32[3,1,64,128]{2,3,1,0:T(8,128)S(1)}, f32[3,1,64,128]{2,3,1,0:T(8,128)S(1)}, u32[]{:S(2)}, u32[]{:S(2)}) collective-permute-start(f32[3,1,64,128]{2,3,1,0:T(8,128)S(1)} %pad_maximum_fusion.9), channel_id=1, source_target_pairs={{0,4},{4,8},{8,12},{12,16},{16,20},{20,24},{24,28},{1,5},{5,9},{9,... | collective-permute-start | bytes 294920 | tf_op jit(solution)/shard_map/ppermute | solution.py:24
where the time goes:
time: 80.4 us; the launch traced here: 79.6 us
  starting transfers between devices  24.5 us (30%)
  local copies, waits for them, and re-layouts  19.2 us (24%)
  blocking collectives  11.9 us (15%)
  matrix products  8.49 us (11%)
  waiting for transfers between devices  7.58 us (9%)
  other arithmetic  5.04 us (6%)
  between operations  2.16 us (3%)
    ppermute x2, starting transfers between devices, with_halo(): before = lax.ppermute(last, axis, up)  9.73 us
    dot_general x22, matrix products, sweep_once(): jnp.einsum('bij,xbjy->xbiy', block_inverse, shaped + coupling, precision=...  7.89 us
    unnamed x32, local copies, waits for them, and re-layouts  7.66 us
    ppermute x2, starting transfers between devices, with_halo(): after = lax.ppermute(leading, axis, down)  6.77 us
    all_to_all x1, blocking collectives, per_device(): lax.all_to_all(outgoing, 'gy', split_axis=3, concat_axis=1, tiled=True)  5.96 us
    all_to_all x1, blocking collectives, per_device(): lax.all_to_all(returned_form, 'gy', split_axis=1, concat_axis=3, tiled=True)  5.96 us
    concatenate x88, local copies, waits for them, and re-layouts, sweep_once(): jnp.concatenate([from_below[:, :, None, :], middle, from_above[:, :, None...  5.81 us
    all_to_all x1, starting transfers between devices, per_device(): lax.all_to_all(outgoing, 'gy', split_axis=3, concat_axis=1, tiled=True)  4.4 us
  transfers between devices with their start and end apart: 6, of which 5 were waited for; matrix products, arithmetic and copies ran while one was open for 2% of the time, Pallas kernels for 0%

commit v1 on v0

--- a/solution.py
+++ b/solution.py
@@ -116,7 +116,19 @@
     for step_index in range(STEPS):
         later_index = STEPS - 1 - step_index
         outgoing = adjoint_v.reshape(row_count, 1, depth_cells, groups, narrow)
-        pieces = lax.all_to_all(outgoing, "gy", split_axis=3, concat_axis=1, tiled=True)
+        ways, here = (lax.axis_size("gy"), lax.axis_index("gy"))
+        width_2 = outgoing.shape[3] // ways
+        shape = list(outgoing.shape)
+        shape[3] = width_2
+        height = shape[1]
+        shape[1] = height * ways
+        full = jnp.zeros(shape, outgoing.dtype)
+        for mask in range(ways):
+            part = lax.dynamic_slice_in_dim(outgoing, (here ^ mask) * width_2, width_2, axis=3)
+            if mask:
+                part = lax.ppermute(part, "gy", [(d, d ^ mask) for d in range(ways)])
+            full = lax.dynamic_update_slice_in_dim(full, part, (here ^ mask) * height, axis=1)
+        pieces = full
         item_count = pieces.shape[0]
         line_cells = pieces.reshape(item_count, groups * depth_cells, narrow)
         solved_lines = line_solve(line_cells, block_rate, block_inverse)

time: 80.4 us -> 76.9 us (0.956)
  blocking collectives: 11.9 us -> 6.76 us
  starting transfers between devices: 24.5 us -> 27 us
  other arithmetic: 5.04 us -> 3.63 us
  waiting for transfers between devices: 7.58 us -> 8.68 us
    ppermute x0 -> x6, starting transfers between devices: none -> 6.09 us  [per_device(): part = lax.ppermute(part, 'gy', [(d, d ^ mask) for d in range(ways)])]
    all_to_all x1 -> x0, blocking collectives: 5.96 us -> none  [per_device(): lax.all_to_all(outgoing, 'gy', split_axis=3, concat_axis=1, tiled=True)]
    all_to_all x1 -> x0, starting transfers between devices: 4.4 us -> none  [per_device(): lax.all_to_all(outgoing, 'gy', split_axis=3, concat_axis=1, tiled=True)]
    all_to_all x2 -> x0, other arithmetic: 1.43 us -> none  [per_device(): lax.all_to_all(outgoing, 'gy', split_axis=3, concat_axis=1, tiled=True)]
    ppermute x0 -> x6, waiting for transfers between devices: none -> 1.12 us  [per_device(): part = lax.ppermute(part, 'gy', [(d, d ^ mask) for d in range(ways)])]
    unnamed x32 -> x28, local copies, waits for them, and re-layouts: 7.66 us -> 6.61 us
    ppermute x2, starting transfers between devices: 6.77 us -> 7.67 us  [with_halo(): after = lax.ppermute(leading, axis, down)]
  transfers between devices with their start and end apart: 6 -> 11, of which waited for: 5 -> 8; matrix products, arithmetic and copies ran while one was open for 2% -> 2% of each run, Pallas kernels for 0% -> 0%
where the time goes in v1:
time: 76.9 us; the launch traced here: 76.3 us
  starting transfers between devices  27 us (35%)
  local copies, waits for them, and re-layouts  18.8 us (24%)
  waiting for transfers between devices  8.68 us (11%)
  matrix products  8.49 us (11%)
  blocking collectives  6.76 us (9%)
  other arithmetic  3.63 us (5%)
  between operations  2.17 us (3%)
    ppermute x2, starting transfers between devices, with_halo(): before = lax.ppermute(last, axis, up)  9.73 us
    dot_general x22, matrix products, sweep_once(): jnp.einsum('bij,xbjy->xbiy', block_inverse, shaped + coupling, precision=...  7.89 us
    ppermute x2, starting transfers between devices, with_halo(): after = lax.ppermute(leading, axis, down)  7.67 us
    all_to_all x1, blocking collectives, per_device(): lax.all_to_all(returned_form, 'gy', split_axis=1, concat_axis=3, tiled=True)  6.76 us
    unnamed x28, local copies, waits for them, and re-layouts  6.61 us
    ppermute x6, starting transfers between devices, per_device(): part = lax.ppermute(part, 'gy', [(d, d ^ mask) for d in range(ways)])  6.09 us
    concatenate x88, local copies, waits for them, and re-layouts, sweep_once(): jnp.concatenate([from_below[:, :, None, :], middle, from_above[:, :, None...  5.81 us
    all_to_all x1, waiting for transfers between devices, per_device(): lax.all_to_all(returned_form, 'gy', split_axis=1, concat_axis=3, tiled=True)  3.6 us
  transfers between devices with their start and end apart: 11, of which 8 were waited for; matrix products, arithmetic and copies ran while one was open for 2% of the time, Pallas kernels for 0%

profile of v1, /device:TPU:1, one launch (start us, length us, event | category | flops | bytes accessed | tf_op | source)
XLA Modules:
  0.0 76.3 jit_solution(15313273844013842778)
XLA Ops:
  0.6 0.8 %copy.79 = f32[1,64,128]{1,2,0:T(8,128)S(1)} copy(f32[1,64,128]{2,1,0:T(8,128)} %param.13) | data formatting | bytes 65536 | tf_op args[0]
  1.6 2.1 %collective-permute-start = (f32[1,1,64,1,32]{2,4,3,1,0:T(8,128)S(1)}, f32[1,1,64,1,32]{2,4,3,1,0:T(8,128)S(1)}, u32[]{:S(2)}, u32[]{:S(2)}) collective-permute-start(f32[1,1,64,1,32]{2,4,3,1,0:T(8,128)S(1)} %get-tuple-element.163), channel_id=1, source_target_pairs={{0,1},{1,0},{2,3},{3,2},{4,5},{5,4},{6,7},{7,6},{8,9},{9,8},{10,11... | collective-permute-start | bytes 24584 | tf_op jit(solution)/shard_map/ppermute | solution.py:129
  3.7 1.2 %collective-permute-start.1 = (f32[1,1,64,1,32]{2,4,3,1,0:T(8,128)S(1)}, f32[1,1,64,1,32]{2,4,3,1,0:T(8,128)S(1)}, u32[]{:S(2)}, u32[]{:S(2)}) collective-permute-start(f32[1,1,64,1,32]{2,4,3,1,0:T(8,128)S(1)} %get-tuple-element.162), channel_id=1, source_target_pairs={{0,2},{1,3},{2,0},{3,1},{4,6},{5,7},{6,4},{7,5},{8,10},{9,11},{10,... | collective-permute-start | bytes 24584 | tf_op jit(solution)/shard_map/ppermute | solution.py:129
  4.9 0.6 fusion.69
  5.6 0.7 copy-done.3
  7.6 0.6 copy-done.4
  9.1 0.7 copy-done
  9.8 0.3 convolution_bitcast_fusion.3
  10.1 9.9 %while.20 = (s32[]{:T(128)}, f32[1,2,128,32]{2,3,1,0:T(8,128)S(1)}, f32[1,2,128,32]{2,3,1,0:T(8,128)S(1)}, f32[2]{0:T(128)S(1)}, f32[2]{0:T(128)S(1)}, /*index=5...) while((s32[]{:T(128)}, f32[1,2,128,32]{2,3,1,0:T(8,128)S(1)}, f32[1,2,128,32]{2,3,1,0:T(8,128)S(1)}, ...), condition=%wide.region_1.2_spmd, body=%wide.region_0.1_spmd.sunk | while | flops 12607618 | bytes 202597 | solution.py:83
  10.1 0.2 slice_reduce_fusion.6
  10.6 0.4 convolution_bitcast_fusion.6
  11.0 0.2 slice_reduce_fusion.6
  11.5 0.4 convolution_bitcast_fusion.6
  11.9 0.2 slice_reduce_fusion.6
  12.4 0.4 convolution_bitcast_fusion.6
  12.8 0.2 slice_reduce_fusion.6
  13.3 0.4 convolution_bitcast_fusion.6
  13.7 0.2 slice_reduce_fusion.6
  14.2 0.4 convolution_bitcast_fusion.6
  14.6 0.2 slice_reduce_fusion.6
  15.1 0.4 convolution_bitcast_fusion.6
  15.5 0.2 slice_reduce_fusion.6
  16.0 0.4 convolution_bitcast_fusion.6
  16.4 0.2 slice_reduce_fusion.6
  16.9 0.4 convolution_bitcast_fusion.6
  17.8 0.4 convolution_bitcast_fusion.6
  18.7 0.4 convolution_bitcast_fusion.6
  19.6 0.4 convolution_bitcast_fusion.6
  20.1 0.7 reshape.979
  20.9 3.6 %all-to-all-start = ((f32[4,1,2048]{2,1,0:T(1,128)}), f32[4,1,2048]{2,1,0:T(1,128)S(1)}, u32[]{:S(2)}, u32[]{:S(2)}) async-start(f32[4,1,2048]{2,1,0:T(1,128)} %reshape.979), calls=%async_computation | async-start | bytes 65536 | tf_op jit(solution)/shard_map/all_to_all | solution.py:136
  24.4 3.6 %all-to-all-done = f32[4,1,2048]{2,1,0:T(1,128)S(1)} async-done(((f32[4,1,2048]{2,1,0:T(1,128)}), f32[4,1,2048]{2,1,0:T(1,128)S(1)}, u32[]{:S(2)}, u32[]{:S(2)}) %all-to-all-start) | async-done | bytes 32800 | tf_op jit(solution)/shard_map/all_to_all | solution.py:136
  28.0 0.5 broadcast.560
  28.5 0.7 reduce.11
  29.4 4.9 %collective-permute-start.3 = (f32[3,1,64,128]{2,3,1,0:T(8,128)S(1)}, f32[3,1,64,128]{2,3,1,0:T(8,128)S(1)}, u32[]{:S(2)}, u32[]{:S(2)}) collective-permute-start(f32[3,1,64,128]{2,3,1,0:T(8,128)S(1)} %pad_maximum_fusion.8), channel_id=1, source_target_pairs={{4,0},{8,4},{12,8},{16,12},{20,16},{24,20},{28,24},{5,1},{9,5},{13... | collective-permute-start | bytes 294920 | tf_op jit(solution)/shard_map/ppermute | solution.py:25
  34.3 3.1 %collective-permute-start.4 = (f32[3,1,64,128]{2,3,1,0:T(8,128)S(1)}, f32[3,1,64,128]{2,3,1,0:T(8,128)S(1)}, u32[]{:S(2)}, u32[]{:S(2)}) collective-permute-start(f32[3,1,64,128]{2,3,1,0:T(8,128)S(1)} %pad_maximum_fusion.8), channel_id=1, source_target_pairs={{0,4},{4,8},{8,12},{12,16},{16,20},{20,24},{24,28},{1,5},{5,9},{9,... | collective-permute-start | bytes 294920 | tf_op jit(solution)/shard_map/ppermute | solution.py:24
  37.6 0.6 copy-done.1
  38.4 0.4 collective-permute-done.3
  38.8 1.2 %collective-permute-done.4 = f32[3,1,64,128]{2,3,1,0:T(8,128)S(1)} collective-permute-done((f32[3,1,64,128]{2,3,1,0:T(8,128)S(1)}, f32[3,1,64,128]{2,3,1,0:T(8,128)S(1)}, u32[]{:S(2)}, u32[]{:S(2)}) %collective-permute-start.4) | collective-permute-done | bytes 98336 | tf_op jit(solution)/shard_map/ppermute | solution.py:24
  40.1 0.4 collective-permute-start.5
  40.6 0.2 collective-permute-start.6
  40.8 2.1 %collective-permute-start.7 = (f32[1,1,64,1,32]{2,4,3,1,0:T(8,128)S(1)}, f32[1,1,64,1,32]{2,4,3,1,0:T(8,128)S(1)}, u32[]{:S(2)}, u32[]{:S(2)}) collective-permute-start(f32[1,1,64,1,32]{2,4,3,1,0:T(8,128)S(1)} %get-tuple-element.154), channel_id=1, source_target_pairs={{0,3},{1,2},{2,1},{3,0},{4,7},{5,6},{6,5},{7,4},{8,11},{9,10},{10,... | collective-permute-start | bytes 24584 | tf_op jit(solution)/shard_map/ppermute | solution.py:129
  43.2 0.2 collective-permute-done.6
  43.4 0.8 %collective-permute-done.7 = f32[1,1,64,1,32]{2,4,3,1,0:T(8,128)S(1)} collective-permute-done((f32[1,1,64,1,32]{2,4,3,1,0:T(8,128)S(1)}, f32[1,1,64,1,32]{2,4,3,1,0:T(8,128)S(1)}, u32[]{:S(2)}, u32[]{:S(2)}) %collective-permute-start.7) | collective-permute-done | bytes 8224 | tf_op jit(solution)/shard_map/ppermute | solution.py:129
  44.6 0.3 convolution_bitcast_fusion.2
  44.9 9.9 %while.21 = (s32[]{:T(128)}, f32[1,2,128,32]{2,3,1,0:T(8,128)S(1)}, f32[1,2,128,32]{2,3,1,0:T(8,128)S(1)}, f32[2]{0:T(128)S(1)}, f32[2]{0:T(128)S(1)}, /*index=5...) while((s32[]{:T(128)}, f32[1,2,128,32]{2,3,1,0:T(8,128)S(1)}, f32[1,2,128,32]{2,3,1,0:T(8,128)S(1)}, ...), condition=%wide.region_6.7_spmd, body=%wide.region_5.6_spmd.sunk | while | flops 12607618 | bytes 202597 | solution.py:83
  45.4 0.4 convolution_bitcast_fusion.7
  46.3 0.4 convolution_bitcast_fusion.7
  47.2 0.4 convolution_bitcast_fusion.7
  48.1 0.4 convolution_bitcast_fusion.7
  49.0 0.4 convolution_bitcast_fusion.7
  49.9 0.4 convolution_bitcast_fusion.7
  50.8 0.4 convolution_bitcast_fusion.7
  51.7 0.4 convolution_bitcast_fusion.7
  52.6 0.4 convolution_bitcast_fusion.7
  53.5 0.4 convolution_bitcast_fusion.7
  54.4 0.4 convolution_bitcast_fusion.7
  55.0 6.8 %all_to_all.30 = f32[4,1,2048]{2,1,0:T(1,128)S(1)} all-to-all(f32[4,1,2048]{2,1,0:T(1,128)S(1)} %reshape.981), channel_id=1, replica_groups=mesh['gx'=8,'gy'=4] {'gy'}, dimensions={0} | all-to-all | bytes 65536 | tf_op jit(solution)/shard_map/all_to_all | solution.py:136
  61.8 0.7 reduce.12
  62.7 2.8 %collective-permute-start.8 = (f32[3,1,64,128]{2,3,1,0:T(8,128)S(1)}, f32[3,1,64,128]{2,3,1,0:T(8,128)S(1)}, u32[]{:S(2)}, u32[]{:S(2)}) collective-permute-start(f32[3,1,64,128]{2,3,1,0:T(8,128)S(1)} %pad_maximum_fusion.9), channel_id=1, source_target_pairs={{4,0},{8,4},{12,8},{16,12},{20,16},{24,20},{28,24},{5,1},{9,5},{13... | collective-permute-start | bytes 294920 | tf_op jit(solution)/shard_map/ppermute | solution.py:25
  65.5 6.6 %collective-permute-start.9 = (f32[3,1,64,128]{2,3,1,0:T(8,128)S(1)}, f32[3,1,64,128]{2,3,1,0:T(8,128)S(1)}, u32[]{:S(2)}, u32[]{:S(2)}) collective-permute-start(f32[3,1,64,128]{2,3,1,0:T(8,128)S(1)} %pad_maximum_fusion.9), channel_id=1, source_target_pairs={{0,4},{4,8},{8,12},{12,16},{16,20},{20,24},{24,28},{1,5},{5,9},{9,... | collective-permute-start | bytes 294920 | tf_op jit(solution)/shard_map/ppermute | solution.py:24
  72.4 1.2 %collective-permute-done.8 = f32[3,1,64,128]{2,3,1,0:T(8,128)S(1)} collective-permute-done((f32[3,1,64,128]{2,3,1,0:T(8,128)S(1)}, f32[3,1,64,128]{2,3,1,0:T(8,128)S(1)}, u32[]{:S(2)}, u32[]{:S(2)}) %collective-permute-start.8) | collective-permute-done | bytes 98336 | tf_op jit(solution)/shard_map/ppermute | solution.py:25
  73.6 1.2 %collective-permute-done.9 = f32[3,1,64,128]{2,3,1,0:T(8,128)S(1)} collective-permute-done((f32[3,1,64,128]{2,3,1,0:T(8,128)S(1)}, f32[3,1,64,128]{2,3,1,0:T(8,128)S(1)}, u32[]{:S(2)}, u32[]{:S(2)}) %collective-permute-start.9) | collective-permute-done | bytes 98336 | tf_op jit(solution)/shard_map/ppermute | solution.py:24
  74.9 0.7 copy.102
  75.6 0.7 copy.103
  (232 shorter events, 13.1 us)
Async XLA Ops:
  1.5 4.1 %copy-start.2 = (bf16[2,1,64,128]{3,2,1,0:T(8,128)(2,1)S(1)}, bf16[2,1,64,128]{3,2,1,0:T(8,128)(2,1)}, u32[]{:S(2)}) copy-start(bf16[2,1,64,128]{3,2,1,0:T(8,128)(2,1)} %param.15) | copy-start | bytes 98308
  1.6 7.0 %collective-permute-start = (f32[1,1,64,1,32]{2,4,3,1,0:T(8,128)S(1)}, f32[1,1,64,1,32]{2,4,3,1,0:T(8,128)S(1)}, u32[]{:S(2)}, u32[]{:S(2)}) collective-permute-start(f32[1,1,64,1,32]{2,4,3,1,0:T(8,128)S(1)} %get-tuple-element.163), channel_id=1, source_target_pairs={{0,1},{1,0},{2,3},{3,2},{4,5},{5,4},{6,7},{7,6},{8,9},{9,8},{10,11... | collective-permute-start | bytes 24584 | tf_op jit(solution)/shard_map/ppermute | solution.py:129
  3.7 1.3 %copy-start.5 = (f32[2]{0:T(128)S(1)}, f32[2]{0:T(128)}, u32[]{:S(2)}) copy-start(f32[2]{0:T(128)} %param.20) | copy-start | bytes 28
  3.7 5.0 %collective-permute-start.1 = (f32[1,1,64,1,32]{2,4,3,1,0:T(8,128)S(1)}, f32[1,1,64,1,32]{2,4,3,1,0:T(8,128)S(1)}, u32[]{:S(2)}, u32[]{:S(2)}) collective-permute-start(f32[1,1,64,1,32]{2,4,3,1,0:T(8,128)S(1)} %get-tuple-element.162), channel_id=1, source_target_pairs={{0,2},{1,3},{2,0},{3,1},{4,6},{5,7},{6,4},{7,5},{8,10},{9,11},{10,... | collective-permute-start | bytes 24584 | tf_op jit(solution)/shard_map/ppermute | solution.py:129
  4.9 0.7 copy-start.6
  4.9 3.8 %collective-permute-start.2 = (f32[1,1,64,1,32]{2,4,3,1,0:T(8,128)S(1)}, f32[1,1,64,1,32]{2,4,3,1,0:T(8,128)S(1)}, u32[]{:S(2)}, u32[]{:S(2)}) collective-permute-start(f32[1,1,64,1,32]{2,4,3,1,0:T(8,128)S(1)} %get-tuple-element.161), channel_id=1, source_target_pairs={{0,3},{1,2},{2,1},{3,0},{4,7},{5,6},{6,5},{7,4},{8,11},{9,10},{10,... | collective-permute-start | bytes 24584 | tf_op jit(solution)/shard_map/ppermute | solution.py:129
  5.6 0.8 copy-start.3
  7.6 0.7 copy-start.4
  7.6 0.7 copy-start.7
  8.8 0.9 %copy-start = (f32[2,128,128]{2,1,0:T(8,128)S(1)}, f32[2,128,128]{2,1,0:T(8,128)}, u32[]{:S(2)}) copy-start(f32[2,128,128]{2,1,0:T(8,128)} %param.21) | copy-start | bytes 393220
  20.9 7.2 %all-to-all-start = ((f32[4,1,2048]{2,1,0:T(1,128)}), f32[4,1,2048]{2,1,0:T(1,128)S(1)}, u32[]{:S(2)}, u32[]{:S(2)}) async-start(f32[4,1,2048]{2,1,0:T(1,128)} %reshape.979), calls=%async_computation | async-start | bytes 65536 | tf_op jit(solution)/shard_map/all_to_all | solution.py:136
  29.4 9.4 %collective-permute-start.3 = (f32[3,1,64,128]{2,3,1,0:T(8,128)S(1)}, f32[3,1,64,128]{2,3,1,0:T(8,128)S(1)}, u32[]{:S(2)}, u32[]{:S(2)}) collective-permute-start(f32[3,1,64,128]{2,3,1,0:T(8,128)S(1)} %pad_maximum_fusion.8), channel_id=1, source_target_pairs={{4,0},{8,4},{12,8},{16,12},{20,16},{24,20},{28,24},{5,1},{9,5},{13... | collective-permute-start | bytes 294920 | tf_op jit(solution)/shard_map/ppermute | solution.py:25
  34.3 5.7 %collective-permute-start.4 = (f32[3,1,64,128]{2,3,1,0:T(8,128)S(1)}, f32[3,1,64,128]{2,3,1,0:T(8,128)S(1)}, u32[]{:S(2)}, u32[]{:S(2)}) collective-permute-start(f32[3,1,64,128]{2,3,1,0:T(8,128)S(1)} %pad_maximum_fusion.8), channel_id=1, source_target_pairs={{0,4},{4,8},{8,12},{12,16},{16,20},{20,24},{24,28},{1,5},{5,9},{9,... | collective-permute-start | bytes 294920 | tf_op jit(solution)/shard_map/ppermute | solution.py:24
  37.5 0.8 %copy-start.1 = (f32[1,64,128]{2,1,0:T(8,128)S(1)}, f32[1,64,128]{2,1,0:T(8,128)}, u32[]{:S(2)}) copy-start(f32[1,64,128]{2,1,0:T(8,128)} %param.14) | copy-start | bytes 98308
  40.1 2.9 %collective-permute-start.5 = (f32[1,1,64,1,32]{2,4,3,1,0:T(8,128)S(1)}, f32[1,1,64,1,32]{2,4,3,1,0:T(8,128)S(1)}, u32[]{:S(2)}, u32[]{:S(2)}) collective-permute-start(f32[1,1,64,1,32]{2,4,3,1,0:T(8,128)S(1)} %get-tuple-element.156), channel_id=1, source_target_pairs={{0,1},{1,0},{2,3},{3,2},{4,5},{5,4},{6,7},{7,6},{8,9},{9,8},{10,11... | collective-permute-start | bytes 24584 | tf_op jit(solution)/shard_map/ppermute | solution.py:129
  40.6 2.8 %collective-permute-start.6 = (f32[1,1,64,1,32]{2,4,3,1,0:T(8,128)S(1)}, f32[1,1,64,1,32]{2,4,3,1,0:T(8,128)S(1)}, u32[]{:S(2)}, u32[]{:S(2)}) collective-permute-start(f32[1,1,64,1,32]{2,4,3,1,0:T(8,128)S(1)} %get-tuple-element.155), channel_id=1, source_target_pairs={{0,2},{1,3},{2,0},{3,1},{4,6},{5,7},{6,4},{7,5},{8,10},{9,11},{10,... | collective-permute-start | bytes 24584 | tf_op jit(solution)/shard_map/ppermute | solution.py:129
  40.8 3.5 %collective-permute-start.7 = (f32[1,1,64,1,32]{2,4,3,1,0:T(8,128)S(1)}, f32[1,1,64,1,32]{2,4,3,1,0:T(8,128)S(1)}, u32[]{:S(2)}, u32[]{:S(2)}) collective-permute-start(f32[1,1,64,1,32]{2,4,3,1,0:T(8,128)S(1)} %get-tuple-element.154), channel_id=1, source_target_pairs={{0,3},{1,2},{2,1},{3,0},{4,7},{5,6},{6,5},{7,4},{8,11},{9,10},{10,... | collective-permute-start | bytes 24584 | tf_op jit(solution)/shard_map/ppermute | solution.py:129
  62.7 10.9 %collective-permute-start.8 = (f32[3,1,64,128]{2,3,1,0:T(8,128)S(1)}, f32[3,1,64,128]{2,3,1,0:T(8,128)S(1)}, u32[]{:S(2)}, u32[]{:S(2)}) collective-permute-start(f32[3,1,64,128]{2,3,1,0:T(8,128)S(1)} %pad_maximum_fusion.9), channel_id=1, source_target_pairs={{4,0},{8,4},{12,8},{16,12},{20,16},{24,20},{28,24},{5,1},{9,5},{13... | collective-permute-start | bytes 294920 | tf_op jit(solution)/shard_map/ppermute | solution.py:25
  65.5 9.2 %collective-permute-start.9 = (f32[3,1,64,128]{2,3,1,0:T(8,128)S(1)}, f32[3,1,64,128]{2,3,1,0:T(8,128)S(1)}, u32[]{:S(2)}, u32[]{:S(2)}) collective-permute-start(f32[3,1,64,128]{2,3,1,0:T(8,128)S(1)} %pad_maximum_fusion.9), channel_id=1, source_target_pairs={{0,4},{4,8},{8,12},{12,16},{16,20},{20,24},{24,28},{1,5},{5,9},{9,... | collective-permute-start | bytes 294920 | tf_op jit(solution)/shard_map/ppermute | solution.py:24
